TPU v7x, 256 devices: a whole 4x4x8 slice. The times are simulated.
256 devices in a mesh: freq: 8 (over y, core), tile: 32 (over z, x).
Axes of the slice: x: 4, y: 4, z: 8, core: 2. Of those that a mesh axis runs over, the one named last changes fastest.
Arguments:
- focus_start: float32 [16, 2, 64, 8192], P('freq', None, None, 'tile'), may hold values from -6 to 6
- v_factor: bfloat16 [16, 32, 32, 64, 2, 256], P('freq', None, 'tile'), may hold values from -0.25 to 0.25
- u_factor: bfloat16 [16, 32, 32, 64, 2, 256], P('freq', 'tile'), may hold values from -0.109375 to 0.109375
- tile_ranks: int32 [16, 32, 32], P('freq'), may hold values from 8 to 64
- onsets: int32 [8192], P('tile'), may hold values from 64 to 512
Outputs:
- focusing: float32 [16, 2, 64, 8192], P('freq', None, None, 'tile')
- upgoing: float32 [16, 2, 64, 8192], P('freq', None, None, 'tile')
All inputs are finite; a program needn't handle non-finite values.
Results may differ from a plain program's by a relative error of at most 0.006.
Values may be sent and summed in bfloat16 or wider, within the bound.
A program may use at most 128 MiB of HBM per device.

v0:
```python
import functools
import math

import jax
import jax.numpy as jnp
import ml_dtypes
import numpy as np
from jax import lax
from jax.experimental import pallas as pl
from jax.experimental.pallas import tpu as pltpu
from jax.sharding import PartitionSpec as P

TILE = 256
RANK = 64
S = 64
NT = 512
ITERS = 2
NF = 16
ZS = 8
XS = 4
TILES = ZS * XS
GROUPS = 8
CHUNKS = 2
SC = S // CHUNKS
HALVES = 2 * ITERS
PHASES = HALVES * CHUNKS
ROWS = TILES * RANK
HALF = TILE // 2
TABLE = 48
MESH = pl.DeviceIdType.MESH
F32 = jnp.float32
BF16 = jnp.bfloat16


def trig_parts():
    orders = np.arange(TABLE)[:, None] - (NF - 1)
    angles = (orders * np.arange(NT)[None, :] % NT) * (2.0 * math.pi / NT)
    rest = np.concatenate([np.cos(angles), np.sin(angles)], axis=0)
    parts = []
    for _ in range(3):
        part = rest.astype(ml_dtypes.bfloat16)
        parts.append(part)
        rest = rest - part.astype(np.float64)
    return np.concatenate(parts, axis=0)


def contract(left, right, left_dim, right_dim):
    return lax.dot_general(
        left, right, (((left_dim,), (right_dim,)), ((), ())), preferred_element_type=F32
    )


def kernel(
    start_ref, v_hbm, u_hbm, onset_ref, trig_ref,
    focus_ref, up_ref,
    v_ref, u_ref, stack, code_out, code_in, turned,
    wave_out, wave_in, gated_out, gated_in, table, gate_rows,
    load_sem, code_send, code_recv, wave_send, wave_recv, gated_send, gated_recv,
):
    me_f = lax.axis_index("freq")
    me_t = lax.axis_index("tile")
    me_z = me_t // XS
    me_x = me_t % XS

    barrier = pltpu.get_barrier_semaphore()
    for step in range(1, GROUPS):
        pl.semaphore_signal(
            barrier, inc=1, device_id=((me_f + step) % GROUPS, me_t), device_id_type=MESH
        )
    for step in range(1, TILES):
        pl.semaphore_signal(
            barrier, inc=1, device_id=(me_f, (me_t + step) % TILES), device_id_type=MESH
        )
    load_v = pltpu.make_async_copy(v_hbm, v_ref, load_sem.at[0])
    load_u = pltpu.make_async_copy(u_hbm, u_ref, load_sem.at[1])
    load_v.start()
    load_u.start()

    def set_stack(chunk, fields, forward):
        for band in range(2):
            real = fields[band][0].astype(BF16)
            imag = fields[band][1].astype(BF16)
            top = band * 2 * SC
            if forward:
                blocks = ((real, -imag), (imag, real))
            else:
                blocks = ((real, imag), (imag, -real))
            for part in range(2):
                rows = slice(top + part * SC, top + (part + 1) * SC)
                stack[chunk, band, rows, 0:TILE] = blocks[part][0]
                stack[chunk, band, rows, TILE : 2 * TILE] = blocks[part][1]

    def send_codes(factor_ref, phase, chunk):
        def group(index, carry):
            ahead = ZS // 2 + ((index + 1) // 2) * (1 - 2 * (index % 2))
            z = (me_z + ahead) % ZS
            first = pl.multiple_of(z * (XS * RANK), XS * RANK)
            rows = pl.ds(first, XS * RANK)
            product = contract(factor_ref[0, rows, :], stack[chunk, 0], 1, 1) + contract(
                factor_ref[1, rows, :], stack[chunk, 1], 1, 1
            )
            code_out[phase, rows, :] = product.astype(BF16)
            for over in (2, 1, 3, 0):
                tile = z * XS + (me_x + over) % XS

                def start(tile=tile):
                    pltpu.make_async_remote_copy(
                        src_ref=code_out.at[phase, pl.ds(pl.multiple_of(tile * RANK, RANK), RANK)],
                        dst_ref=code_in.at[phase, pl.ds(pl.multiple_of(me_t * RANK, RANK), RANK)],
                        send_sem=code_send.at[phase],
                        recv_sem=code_recv.at[phase],
                        device_id=(me_f, tile),
                        device_id_type=MESH,
                    ).start()

                if over:
                    start()
                else:
                    pl.when(index < ZS - 1)(start)
            return carry

        lax.fori_loop(0, ZS, group, 0)
        own = pl.ds(pl.multiple_of(me_t * RANK, RANK), RANK)
        code_in[phase, own, :] = code_out[phase, own, :]

    def wait_bytes(ref, sem):
        pltpu.make_async_copy(ref, ref, sem).wait()

    def image(factor_ref, phase, forward):
        wait_bytes(code_in.at[phase, pl.ds(0, ROWS - RANK)], code_recv.at[phase])
        turned[...] = code_in[phase].T
        sign = 1.0 if forward else -1.0
        for band in range(2):
            product = contract(
                turned[band * 2 * SC : (band + 1) * 2 * SC, :], factor_ref[band], 1, 0
            )
            real = product[:SC, :TILE] - sign * product[SC:, TILE:]
            imag = product[SC:, :TILE] + sign * product[:SC, TILE:]
            for group in range(GROUPS):
                rows = slice((group // 2) * 8, (group // 2 + 1) * 8)
                lanes = slice((group % 2) * HALF, (group % 2 + 1) * HALF)
                wave_out[phase, group, band * 2] = real[rows, lanes]
                wave_out[phase, group, band * 2 + 1] = imag[rows, lanes]

    def exchange(source, target, send, recv, phase):
        for step in (4, 5, 3, 2, 6, 7, 1):
            peer = (me_f + step) % GROUPS
            pltpu.make_async_remote_copy(
                src_ref=source.at[phase, peer],
                dst_ref=target.at[phase, me_f],
                send_sem=send.at[phase],
                recv_sem=recv.at[phase],
                device_id=(peer, me_t),
                device_id_type=MESH,
            ).start()
        target[phase, me_f] = source[phase, me_f]
        wait_bytes(target.at[phase, pl.ds(0, GROUPS - 1)], recv.at[phase])

    def gate(phase):
        waves = [wave_in[phase, index // 4, index % 4] for index in range(2 * NF)]

        def row(index, carry):
            total = None
            for part in range(2):
                for wave in range(NF):
                    weight = gate_rows[index, part, wave : wave + 1, :]
                    term = weight * waves[2 * wave + part]
                    total = term if total is None else total + term
            gated_out[phase, index // 4, index % 4] = total
            return carry

        lax.fori_loop(0, 2 * NF, row, 0)

    def gated_fields(phase):
        return [
            [
                jnp.concatenate(
                    [
                        jnp.concatenate(
                            [gated_in[phase, 2 * up + side, band * 2 + part] for side in range(2)], axis=1
                        )
                        for up in range(GROUPS // 2)
                    ],
                    axis=0,
                )
                for part in range(2)
            ]
            for band in range(2)
        ]

    def start_fields(chunk):
        rows = slice(chunk * SC, (chunk + 1) * SC)
        return [[start_ref[band, part, rows, :] for part in range(2)] for band in range(2)]

    stack[...] = jnp.zeros_like(stack)
    for chunk in range(CHUNKS):
        set_stack(chunk, start_fields(chunk), True)
    load_v.wait()
    pl.semaphore_wait(barrier, GROUPS + TILES - 2)
    for chunk in range(CHUNKS):
        send_codes(v_ref, chunk, chunk)

    limits = onset_ref[pl.ds(me_f % 2, 1), :]
    window = jnp.where(lax.broadcasted_iota(jnp.int32, (NT, HALF), 0) < limits, 1.0, 0.0).astype(BF16)
    sums = contract(trig_ref[...], window, 1, 0)
    table[...] = (sums[: 2 * TABLE] + sums[2 * TABLE : 4 * TABLE] + sums[4 * TABLE :]) * (1.0 / NT)
    for wave in range(NF):
        low, high = NF - 1 - wave, NF + 1 + wave
        cos_low = table[low : low + NF, :]
        cos_high = table[high : high + NF, :]
        sin_low = table[TABLE + low : TABLE + low + NF, :]
        sin_high = table[TABLE + high : TABLE + high + NF, :]
        gate_rows[2 * wave, 0] = cos_low + cos_high
        gate_rows[2 * wave, 1] = sin_high + sin_low
        gate_rows[2 * wave + 1, 0] = sin_high - sin_low
        gate_rows[2 * wave + 1, 1] = cos_low - cos_high
    load_u.wait()

    for half in range(HALVES):
        forward = half % 2 == 0
        for chunk in range(CHUNKS):
            phase = half * CHUNKS + chunk
            rows = slice(chunk * SC, (chunk + 1) * SC)
            image(u_ref if forward else v_ref, phase, forward)
            exchange(wave_out, wave_in, wave_send, wave_recv, phase)
            gate(phase)
            exchange(gated_out, gated_in, gated_send, gated_recv, phase)
            fields = gated_fields(phase)
            if not forward:
                begun = start_fields(chunk)
                fields = [[begun[band][part] + fields[band][part] for part in range(2)] for band in range(2)]
            if half + 1 < HALVES:
                set_stack(chunk, fields, not forward)
                send_codes(u_ref if forward else v_ref, phase + CHUNKS, chunk)
            if half >= HALVES - 2:
                target = up_ref if forward else focus_ref
                for band in range(2):
                    for part in range(2):
                        target[band, part, rows, :] = fields[band][part]
    for phase in range(PHASES):
        wait_bytes(code_out.at[phase, pl.ds(0, ROWS - RANK)], code_send.at[phase])
        wait_bytes(wave_out.at[phase, pl.ds(0, GROUPS - 1)], wave_send.at[phase])
        wait_bytes(gated_out.at[phase, pl.ds(0, GROUPS - 1)], gated_send.at[phase])


def per_device(trig, focus_start, v_factor, u_factor, tile_ranks, onsets):
    own_tile = lax.axis_index("tile")
    column_ranks = lax.dynamic_slice_in_dim(tile_ranks, own_tile, 1, 2)[:, :, 0]
    row_ranks = lax.dynamic_slice_in_dim(tile_ranks, own_tile, 1, 1)[:, 0, :]
    levels = lax.iota(jnp.int32, RANK)

    def packed(factor, ranks):
        live = levels[None, None, :] < ranks[:, :, None]
        blocks = factor.reshape(2, TILES, RANK, 2, TILE)
        blocks = jnp.where(live[..., None, None], blocks, jnp.zeros_like(blocks))
        return blocks.reshape(2, ROWS, 2 * TILE)

    vmem = pl.BlockSpec(memory_space=pltpu.VMEM)
    anywhere = pl.BlockSpec(memory_space=pl.ANY)
    dma = pltpu.SemaphoreType.DMA
    field = jax.ShapeDtypeStruct((2, 2, S, TILE), F32)
    return pl.pallas_call(
        kernel,
        out_shape=(field, field),
        in_specs=[vmem, anywhere, anywhere, vmem, vmem],
        out_specs=(vmem, vmem),
        scratch_shapes=[
            pltpu.VMEM((2, ROWS, 2 * TILE), BF16),
            pltpu.VMEM((2, ROWS, 2 * TILE), BF16),
            pltpu.VMEM((CHUNKS, 2, 4 * SC, 2 * TILE), BF16),
            pltpu.VMEM((PHASES, ROWS, 4 * SC), BF16),
            pltpu.VMEM((PHASES, ROWS, 4 * SC), BF16),
            pltpu.VMEM((4 * SC, ROWS), BF16),
            pltpu.VMEM((PHASES, GROUPS, 4, 8, HALF), F32),
            pltpu.VMEM((PHASES, GROUPS, 4, 8, HALF), F32),
            pltpu.VMEM((PHASES, GROUPS, 4, 8, HALF), F32),
            pltpu.VMEM((PHASES, GROUPS, 4, 8, HALF), F32),
            pltpu.VMEM((2 * TABLE, HALF), F32),
            pltpu.VMEM((2 * NF, 2, NF, HALF), F32),
            dma((2,)),
            dma((PHASES,)),
            dma((PHASES,)),
            dma((PHASES,)),
            dma((PHASES,)),
            dma((PHASES,)),
            dma((PHASES,)),
        ],
        compiler_params=pltpu.CompilerParams(collective_id=0, has_side_effects=True),
    )(
        focus_start,
        packed(v_factor, column_ranks),
        packed(u_factor, row_ranks),
        onsets.reshape(2, HALF),
        trig,
    )


def solution(mesh):
    placed = (
        P("freq", None, None, "tile"),
        P("freq", None, "tile", None, None, None),
        P("freq", "tile", None, None, None, None),
        P("freq", None, None),
        P("tile"),
    )
    trig = trig_parts()

    def body(*args):
        return per_device(jnp.asarray(trig), *args)

    return jax.shard_map(
        body,
        mesh=mesh,
        in_specs=placed,
        out_specs=(P("freq", None, None, "tile"), P("freq", None, None, "tile")),
        check_vma=False,
    )
```

profile of v0, /device:TPU:1, one launch (start us, length us, event | category | flops | bytes accessed | tf_op | source)
XLA Modules:
  0.0 154.2 jit_solution(283322178870098413)
XLA Ops:
  0.6 0.0 copy-start
  0.6 0.7 copy-done
  1.4 0.2 dynamic-slice_reduce_fusion
  1.6 0.1 lt.55
  1.7 0.1 lt.59
  1.7 0.1 lt.60
  1.8 0.1 lt.63
  1.9 0.1 lt.64
  2.0 7.6 %reshape.30 = bf16[2,2048,512]{2,1,0:T(8,128)(2,1)} reshape(bf16[2,32,1,64,2,256]{5,4,3,2,1,0:T(2,128)(2,1)} %param.7) | data formatting | bytes 8388608 | tf_op jit(solution)/shard_map/reshape | solution.py:254
  9.6 7.6 %reshape.31 = bf16[2,2048,512]{2,1,0:T(8,128)(2,1)} reshape(bf16[2,1,32,64,2,256]{5,4,3,2,1,0:T(2,128)(2,1)} %param.8) | data formatting | bytes 8388608 | tf_op jit(solution)/shard_map/reshape | solution.py:254
  17.2 7.3 %broadcast_select_fusion = (bf16[2,2048,512]{2,1,0:T(8,128)(2,1)}, bf16[2,2048,512]{2,1,0:T(8,128)(2,1)}) fusion(bf16[2,2048,512]{2,1,0:T(8,128)(2,1)} %reshape.31, pred[2,2048]{1,0:T(4,128)(4,1)S(1)} %get-tuple-element.2, bf16[2,2048,512]{2,1,0:T(8,128)(2,1)} %reshape.30, pred[2,2048]{1,0:T(4,128)(4,1)S(1)} %get-tuple-element.3), kind=kLoop, calls=%fused_computation | loop fusion | flops 4194304 | bytes 16785408 | tf_op jit(solution)/shard_map/jit(_where)/select_n | solution.py:255
  24.5 126.3 %shard_map.77 = (f32[2,2,64,256]{3,2,1,0:T(8,128)}, f32[2,2,64,256]{3,2,1,0:T(8,128)}) custom-call(f32[2,2,64,256]{3,2,1,0:T(8,128)} %start_ref.1, bf16[2,2048,512]{2,1,0:T(8,128)(2,1)} %get-tuple-element.5.v_hbm, bf16[2,2048,512]{2,1,0:T(8,128)(2,1)} %get-tuple-element.4.u_hbm, s32[2,128]{1,0:T(2,128)} %bitcast.3, bf16[288,512]{1,0:T(8,128)(2,1)} %constant.12.clone.trig_ref), custom_call_target="tpu_custom_call" | custom-call | tf_op jit(solution)/shard_map/pallas_call | solution.py:262
  150.8 1.7 %copy.10 = f32[2,2,64,256]{3,2,1,0:T(8,128)} copy(f32[2,2,64,256]{3,2,1,0:T(8,128)} %get-tuple-element.8) | data formatting | bytes 524288
  152.5 1.7 %copy.11 = f32[2,2,64,256]{3,2,1,0:T(8,128)} copy(f32[2,2,64,256]{3,2,1,0:T(8,128)} %get-tuple-element.9) | data formatting | bytes 524288
  (3 shorter events, 0.0 us)
Async XLA Ops:
  0.6 0.8 copy-start
where the time goes:
time: 155 us; the launch traced here: 154 us
  Pallas kernels  126 us (81%)
  local copies, waits for them, and re-layouts  19.9 us (13%)
  other arithmetic  7.34 us (5%)
    pallas_call x1, Pallas kernels, per_device(): pl.pallas_call(kernel, out_shape=(field, field), in_specs=[vmem, anywhere...  126 us
    reshape x2, local copies, waits for them, and re-layouts, packed(): blocks = factor.reshape(2, TILES, RANK, 2, TILE)  15.2 us
    select_n x1, other arithmetic, packed(): blocks = jnp.where(live[..., None, None], blocks, jnp.zeros_like(blocks))  7.31 us
    unnamed x4, local copies, waits for them, and re-layouts  4.1 us

commit v1 on v0

--- a/solution.py
+++ b/solution.py
@@ -51,9 +51,9 @@
 
 
 def kernel(
-    start_ref, v_hbm, u_hbm, onset_ref, trig_ref,
+    start_ref, v_hbm, u_hbm, rank_ref, onset_ref, trig_ref,
     focus_ref, up_ref,
-    v_ref, u_ref, stack, code_out, code_in, turned,
+    v_raw, u_raw, v_ref, u_ref, spread, stack, code_out, code_in, turned,
     wave_out, wave_in, gated_out, gated_in, table, gate_rows,
     load_sem, code_send, code_recv, wave_send, wave_recv, gated_send, gated_recv,
 ):
@@ -71,8 +71,8 @@
         pl.semaphore_signal(
             barrier, inc=1, device_id=(me_f, (me_t + step) % TILES), device_id_type=MESH
         )
-    load_v = pltpu.make_async_copy(v_hbm, v_ref, load_sem.at[0])
-    load_u = pltpu.make_async_copy(u_hbm, u_ref, load_sem.at[1])
+    load_v = pltpu.make_async_copy(v_hbm, v_raw, load_sem.at[0])
+    load_u = pltpu.make_async_copy(u_hbm, u_raw, load_sem.at[1])
     load_v.start()
     load_u.start()
 
@@ -90,10 +90,24 @@
                 stack[chunk, band, rows, 0:TILE] = blocks[part][0]
                 stack[chunk, band, rows, TILE : 2 * TILE] = blocks[part][1]
 
-    def send_codes(factor_ref, phase, chunk):
+    def unpack(raw, factor_ref, tile, slot, rank_of):
+        for band in range(2):
+            live = lax.broadcasted_iota(jnp.int32, (RANK, HALF), 0) < rank_of(band, tile)
+            spread[slot, band] = raw[band, tile].astype(F32)
+            rows = pl.ds(pl.multiple_of(tile * RANK, RANK), RANK)
+            for side in range(2):
+                for part in range(2):
+                    piece = spread[slot, band, pl.ds(2 * side + part, RANK, stride=4), :]
+                    piece = jnp.where(live, piece, 0.0).astype(BF16)
+                    left = part * TILE + side * HALF
+                    factor_ref[band, rows, left : left + HALF] = piece
+
+    def send_codes(factor_ref, phase, chunk, prepare=None):
         def group(index, carry):
             ahead = ZS // 2 + ((index + 1) // 2) * (1 - 2 * (index % 2))
             z = (me_z + ahead) % ZS
+            if prepare is not None:
+                prepare(z)
             first = pl.multiple_of(z * (XS * RANK), XS * RANK)
             rows = pl.ds(first, XS * RANK)
             product = contract(factor_ref[0, rows, :], stack[chunk, 0], 1, 1) + contract(
@@ -197,7 +211,18 @@
         set_stack(chunk, start_fields(chunk), True)
     load_v.wait()
     pl.semaphore_wait(barrier, GROUPS + TILES - 2)
-    for chunk in range(CHUNKS):
+
+    def prepare_v(z):
+        for over in range(XS):
+            unpack(v_raw, v_ref, z * XS + over, over, lambda band, tile: rank_ref[band, tile, me_t])
+
+    def prepare_u(z, carry):
+        for over in range(XS):
+            unpack(u_raw, u_ref, z * XS + over, over, lambda band, tile: rank_ref[band, me_t, tile])
+        return carry
+
+    send_codes(v_ref, 0, 0, prepare_v)
+    for chunk in range(1, CHUNKS):
         send_codes(v_ref, chunk, chunk)
 
     limits = onset_ref[pl.ds(me_f % 2, 1), :]
@@ -215,6 +240,7 @@
         gate_rows[2 * wave + 1, 0] = sin_high - sin_low
         gate_rows[2 * wave + 1, 1] = cos_low - cos_high
     load_u.wait()
+    lax.fori_loop(0, ZS, prepare_u, 0)
 
     for half in range(HALVES):
         forward = half % 2 == 0
@@ -244,16 +270,9 @@
 
 
 def per_device(trig, focus_start, v_factor, u_factor, tile_ranks, onsets):
-    own_tile = lax.axis_index("tile")
-    column_ranks = lax.dynamic_slice_in_dim(tile_ranks, own_tile, 1, 2)[:, :, 0]
-    row_ranks = lax.dynamic_slice_in_dim(tile_ranks, own_tile, 1, 1)[:, 0, :]
-    levels = lax.iota(jnp.int32, RANK)
-
-    def packed(factor, ranks):
-        live = levels[None, None, :] < ranks[:, :, None]
-        blocks = factor.reshape(2, TILES, RANK, 2, TILE)
-        blocks = jnp.where(live[..., None, None], blocks, jnp.zeros_like(blocks))
-        return blocks.reshape(2, ROWS, 2 * TILE)
+    def split_lanes(factor):
+        blocks = factor.reshape(2, TILES, RANK, 2, 2, HALF)
+        return blocks.transpose(0, 1, 2, 4, 3, 5).reshape(2, TILES, 4 * RANK, HALF)
 
     vmem = pl.BlockSpec(memory_space=pltpu.VMEM)
     anywhere = pl.BlockSpec(memory_space=pl.ANY)
@@ -262,11 +281,14 @@
     return pl.pallas_call(
         kernel,
         out_shape=(field, field),
-        in_specs=[vmem, anywhere, anywhere, vmem, vmem],
+        in_specs=[vmem, anywhere, anywhere, pl.BlockSpec(memory_space=pltpu.SMEM), vmem, vmem],
         out_specs=(vmem, vmem),
         scratch_shapes=[
+            pltpu.VMEM((2, TILES, 4 * RANK, HALF), BF16),
+            pltpu.VMEM((2, TILES, 4 * RANK, HALF), BF16),
             pltpu.VMEM((2, ROWS, 2 * TILE), BF16),
             pltpu.VMEM((2, ROWS, 2 * TILE), BF16),
+            pltpu.VMEM((XS, 2, 4 * RANK, HALF), F32),
             pltpu.VMEM((CHUNKS, 2, 4 * SC, 2 * TILE), BF16),
             pltpu.VMEM((PHASES, ROWS, 4 * SC), BF16),
             pltpu.VMEM((PHASES, ROWS, 4 * SC), BF16),
@@ -288,8 +310,9 @@
         compiler_params=pltpu.CompilerParams(collective_id=0, has_side_effects=True),
     )(
         focus_start,
-        packed(v_factor, column_ranks),
-        packed(u_factor, row_ranks),
+        split_lanes(v_factor),
+        split_lanes(u_factor),
+        tile_ranks,
         onsets.reshape(2, HALF),
         trig,
     )

time: 155 us -> 131 us (0.85)
  local copies, waits for them, and re-layouts: 19.9 us -> 3.35 us
  other arithmetic: 7.34 us -> 0 us
    reshape x2 -> x0, local copies, waits for them, and re-layouts: 15.2 us -> none  [packed(): blocks = factor.reshape(2, TILES, RANK, 2, TILE)]
    select_n x1 -> x0, other arithmetic: 7.31 us -> none  [packed(): blocks = jnp.where(live[..., None, None], blocks, jnp.zeros_like(blocks))]
    unnamed x4 -> x2, local copies, waits for them, and re-layouts: 4.1 us -> 3.35 us
where the time goes in v1:
time: 131 us
  Pallas kernels  127 us (97%)
  local copies, waits for them, and re-layouts  3.35 us (3%)
    pallas_call x1, Pallas kernels, per_device(): pl.pallas_call(kernel, out_shape=(field, field), in_specs=[vmem, anywhere...  127 us
    unnamed x2, local copies, waits for them, and re-layouts  3.35 us

profile of v1, /device:TPU:1, one launch (start us, length us, event | category | flops | bytes accessed | tf_op | source)
XLA Modules:
  0.0 130.7 jit_solution(12674550319910079065)
XLA Ops:
  0.6 126.7 %shard_map.77 = (f32[2,2,64,256]{3,2,1,0:T(8,128)}, f32[2,2,64,256]{3,2,1,0:T(8,128)}) custom-call(f32[2,2,64,256]{3,2,1,0:T(8,128)} %start_ref.1, bf16[2,32,256,128]{3,2,1,0:T(8,128)(2,1)} %bitcast.11, bf16[2,32,256,128]{3,2,1,0:T(8,128)(2,1)} %bitcast.12, s32[2,32,32]{2,1,0:T(8,128)} %rank_ref.1, s32[2,128]{1,0:T(2,128)} %bitcast.13, ...), custom_call_target="tpu_custom_call" | custom-call | tf_op jit(solution)/shard_map/pallas_call | solution.py:281
  127.3 1.7 %copy.12 = f32[2,2,64,256]{3,2,1,0:T(8,128)} copy(f32[2,2,64,256]{3,2,1,0:T(8,128)} %get-tuple-element.4) | data formatting | bytes 524288
  129.0 1.7 %copy.13 = f32[2,2,64,256]{3,2,1,0:T(8,128)} copy(f32[2,2,64,256]{3,2,1,0:T(8,128)} %get-tuple-element.5) | data formatting | bytes 524288

commit v2 on v1

--- a/solution.py
+++ b/solution.py
@@ -51,9 +51,9 @@
 
 
 def kernel(
-    start_ref, v_hbm, u_hbm, rank_ref, onset_ref, trig_ref,
+    start_hbm, v_hbm, u_hbm, rank_ref, onset_ref, trig_hbm,
     focus_ref, up_ref,
-    v_raw, u_raw, v_ref, u_ref, spread, stack, code_out, code_in, turned,
+    start_ref, trig_ref, v_raw, u_raw, v_ref, u_ref, spread, stack, code_out, code_in, turned,
     wave_out, wave_in, gated_out, gated_in, table, gate_rows,
     load_sem, code_send, code_recv, wave_send, wave_recv, gated_send, gated_recv,
 ):
@@ -73,8 +73,10 @@
         )
     load_v = pltpu.make_async_copy(v_hbm, v_raw, load_sem.at[0])
     load_u = pltpu.make_async_copy(u_hbm, u_raw, load_sem.at[1])
-    load_v.start()
-    load_u.start()
+    load_start = pltpu.make_async_copy(start_hbm, start_ref, load_sem.at[2])
+    load_trig = pltpu.make_async_copy(trig_hbm, trig_ref, load_sem.at[3])
+    for load in (load_start, load_v, load_trig, load_u):
+        load.start()
 
     def set_stack(chunk, fields, forward):
         for band in range(2):
@@ -153,8 +155,8 @@
             for group in range(GROUPS):
                 rows = slice((group // 2) * 8, (group // 2 + 1) * 8)
                 lanes = slice((group % 2) * HALF, (group % 2 + 1) * HALF)
-                wave_out[phase, group, band * 2] = real[rows, lanes]
-                wave_out[phase, group, band * 2 + 1] = imag[rows, lanes]
+                pair = jnp.concatenate([real[rows, lanes], imag[rows, lanes]], axis=0)
+                wave_out[phase, group, band] = pair.astype(BF16)
 
     def exchange(source, target, send, recv, phase):
         for step in (4, 5, 3, 2, 6, 7, 1):
@@ -171,42 +173,46 @@
         wait_bytes(target.at[phase, pl.ds(0, GROUPS - 1)], recv.at[phase])
 
     def gate(phase):
-        waves = [wave_in[phase, index // 4, index % 4] for index in range(2 * NF)]
-
-        def row(index, carry):
-            total = None
-            for part in range(2):
+        waves = []
+        for index in range(NF):
+            pair = wave_in[phase, index // 2, index % 2].astype(F32)
+            waves.append((pair[:8], pair[8:]))
+
+        def rows(index, carry):
+            results = []
+            for kind in range(2):
+                totals = [None] * 4
                 for wave in range(NF):
-                    weight = gate_rows[index, part, wave : wave + 1, :]
-                    term = weight * waves[2 * wave + part]
-                    total = term if total is None else total + term
-            gated_out[phase, index // 4, index % 4] = total
+                    for part in range(2):
+                        weight = gate_rows[2 * index + kind, part, wave : wave + 1, :]
+                        term = weight * waves[wave][part]
+                        lane = 2 * (wave % 2) + part
+                        totals[lane] = term if totals[lane] is None else totals[lane] + term
+                results.append((totals[0] + totals[1]) + (totals[2] + totals[3]))
+            gated_out[phase, index // 2, index % 2] = jnp.concatenate(results, axis=0).astype(BF16)
             return carry
 
-        lax.fori_loop(0, 2 * NF, row, 0)
+        lax.fori_loop(0, NF, rows, 0)
 
     def gated_fields(phase):
-        return [
-            [
+        def field(band, part):
+            part_rows = slice(part * 8, part * 8 + 8)
+            bands = [
                 jnp.concatenate(
-                    [
-                        jnp.concatenate(
-                            [gated_in[phase, 2 * up + side, band * 2 + part] for side in range(2)], axis=1
-                        )
-                        for up in range(GROUPS // 2)
-                    ],
-                    axis=0,
+                    [gated_in[phase, 2 * up + side, band].astype(F32)[part_rows] for side in range(2)], axis=1
                 )
-                for part in range(2)
+                for up in range(GROUPS // 2)
             ]
-            for band in range(2)
-        ]
+            return jnp.concatenate(bands, axis=0)
+
+        return [[field(band, part) for part in range(2)] for band in range(2)]
 
     def start_fields(chunk):
         rows = slice(chunk * SC, (chunk + 1) * SC)
         return [[start_ref[band, part, rows, :] for part in range(2)] for band in range(2)]
 
     stack[...] = jnp.zeros_like(stack)
+    load_start.wait()
     for chunk in range(CHUNKS):
         set_stack(chunk, start_fields(chunk), True)
     load_v.wait()
@@ -225,6 +231,7 @@
     for chunk in range(1, CHUNKS):
         send_codes(v_ref, chunk, chunk)
 
+    load_trig.wait()
     limits = onset_ref[pl.ds(me_f % 2, 1), :]
     window = jnp.where(lax.broadcasted_iota(jnp.int32, (NT, HALF), 0) < limits, 1.0, 0.0).astype(BF16)
     sums = contract(trig_ref[...], window, 1, 0)
@@ -277,13 +284,15 @@
     vmem = pl.BlockSpec(memory_space=pltpu.VMEM)
     anywhere = pl.BlockSpec(memory_space=pl.ANY)
     dma = pltpu.SemaphoreType.DMA
-    field = jax.ShapeDtypeStruct((2, 2, S, TILE), F32)
+    field = pltpu.VMEM((2, 2, S, TILE), F32)
     return pl.pallas_call(
         kernel,
         out_shape=(field, field),
-        in_specs=[vmem, anywhere, anywhere, pl.BlockSpec(memory_space=pltpu.SMEM), vmem, vmem],
+        in_specs=[anywhere, anywhere, anywhere, pl.BlockSpec(memory_space=pltpu.SMEM), vmem, anywhere],
         out_specs=(vmem, vmem),
         scratch_shapes=[
+            pltpu.VMEM((2, 2, S, TILE), F32),
+            pltpu.VMEM((6 * TABLE, NT), BF16),
             pltpu.VMEM((2, TILES, 4 * RANK, HALF), BF16),
             pltpu.VMEM((2, TILES, 4 * RANK, HALF), BF16),
             pltpu.VMEM((2, ROWS, 2 * TILE), BF16),
@@ -293,13 +302,13 @@
             pltpu.VMEM((PHASES, ROWS, 4 * SC), BF16),
             pltpu.VMEM((PHASES, ROWS, 4 * SC), BF16),
             pltpu.VMEM((4 * SC, ROWS), BF16),
-            pltpu.VMEM((PHASES, GROUPS, 4, 8, HALF), F32),
-            pltpu.VMEM((PHASES, GROUPS, 4, 8, HALF), F32),
-            pltpu.VMEM((PHASES, GROUPS, 4, 8, HALF), F32),
-            pltpu.VMEM((PHASES, GROUPS, 4, 8, HALF), F32),
+            pltpu.VMEM((PHASES, GROUPS, 2, 16, HALF), BF16),
+            pltpu.VMEM((PHASES, GROUPS, 2, 16, HALF), BF16),
+            pltpu.VMEM((PHASES, GROUPS, 2, 16, HALF), BF16),
+            pltpu.VMEM((PHASES, GROUPS, 2, 16, HALF), BF16),
             pltpu.VMEM((2 * TABLE, HALF), F32),
             pltpu.VMEM((2 * NF, 2, NF, HALF), F32),
-            dma((2,)),
+            dma((4,)),
             dma((PHASES,)),
             dma((PHASES,)),
             dma((PHASES,)),

time: 131 us -> 122 us (0.931)
  Pallas kernels: 127 us -> 120 us
  local copies, waits for them, and re-layouts: 3.35 us -> 1.41 us
    pallas_call x1, Pallas kernels: 127 us -> 120 us  [per_device(): pl.pallas_call(kernel, out_shape=(field, field), in_specs=[anywhere, anyw...]
    unnamed x2, local copies, waits for them, and re-layouts: 3.35 us -> 1.41 us
where the time goes in v2:
time: 122 us
  Pallas kernels  120 us (98%)
  local copies, waits for them, and re-layouts  1.41 us (1%)
    pallas_call x1, Pallas kernels, per_device(): pl.pallas_call(kernel, out_shape=(field, field), in_specs=[anywhere, anyw...  120 us

profile of v2, /device:TPU:1, one launch (start us, length us, event | category | flops | bytes accessed | tf_op | source)
XLA Modules:
  0.0 122.1 jit_solution(14730193288520295548)
XLA Ops:
  0.6 120.1 %shard_map.77 = (f32[2,2,64,256]{3,2,1,0:T(8,128)S(1)}, f32[2,2,64,256]{3,2,1,0:T(8,128)S(1)}) custom-call(f32[2,2,64,256]{3,2,1,0:T(8,128)} %start_hbm.1, bf16[2,32,256,128]{3,2,1,0:T(8,128)(2,1)} %bitcast.11, bf16[2,32,256,128]{3,2,1,0:T(8,128)(2,1)} %bitcast.12, s32[2,32,32]{2,1,0:T(8,128)} %rank_ref.1, s32[2,128]{1,0:T(2,128)} %bitcast.13, ...), custom_call_target="tpu_custom_call" | custom-call | tf_op jit(solution)/shard_map/pallas_call | solution.py:288
  120.7 0.7 copy.12
  121.4 0.7 copy.13

commit v3 on v2

--- a/solution.py
+++ b/solution.py
@@ -105,37 +105,37 @@
                     factor_ref[band, rows, left : left + HALF] = piece
 
     def send_codes(factor_ref, phase, chunk, prepare=None):
-        def group(index, carry):
-            ahead = ZS // 2 + ((index + 1) // 2) * (1 - 2 * (index % 2))
-            z = (me_z + ahead) % ZS
-            if prepare is not None:
-                prepare(z)
-            first = pl.multiple_of(z * (XS * RANK), XS * RANK)
-            rows = pl.ds(first, XS * RANK)
-            product = contract(factor_ref[0, rows, :], stack[chunk, 0], 1, 1) + contract(
-                factor_ref[1, rows, :], stack[chunk, 1], 1, 1
-            )
-            code_out[phase, rows, :] = product.astype(BF16)
+        def pair(index, carry):
+            planes = ((me_z + ZS // 2 - index) % ZS, (me_z + ZS // 2 + 1 + index) % ZS)
+            for z in planes:
+                if prepare is not None:
+                    prepare(z)
+                rows = pl.ds(pl.multiple_of(z * (XS * RANK), XS * RANK), XS * RANK)
+                product = contract(factor_ref[0, rows, :], stack[chunk, 0], 1, 1) + contract(
+                    factor_ref[1, rows, :], stack[chunk, 1], 1, 1
+                )
+                code_out[phase, rows, :] = product.astype(BF16)
             for over in (2, 1, 3, 0):
-                tile = z * XS + (me_x + over) % XS
-
-                def start(tile=tile):
-                    pltpu.make_async_remote_copy(
-                        src_ref=code_out.at[phase, pl.ds(pl.multiple_of(tile * RANK, RANK), RANK)],
-                        dst_ref=code_in.at[phase, pl.ds(pl.multiple_of(me_t * RANK, RANK), RANK)],
-                        send_sem=code_send.at[phase],
-                        recv_sem=code_recv.at[phase],
-                        device_id=(me_f, tile),
-                        device_id_type=MESH,
-                    ).start()
-
-                if over:
-                    start()
-                else:
-                    pl.when(index < ZS - 1)(start)
+                for side, z in enumerate(planes):
+                    tile = z * XS + (me_x + over) % XS
+
+                    def start(tile=tile):
+                        pltpu.make_async_remote_copy(
+                            src_ref=code_out.at[phase, pl.ds(pl.multiple_of(tile * RANK, RANK), RANK)],
+                            dst_ref=code_in.at[phase, pl.ds(pl.multiple_of(me_t * RANK, RANK), RANK)],
+                            send_sem=code_send.at[phase],
+                            recv_sem=code_recv.at[phase],
+                            device_id=(me_f, tile),
+                            device_id_type=MESH,
+                        ).start()
+
+                    if over or not side:
+                        start()
+                    else:
+                        pl.when(index < ZS // 2 - 1)(start)
             return carry
 
-        lax.fori_loop(0, ZS, group, 0)
+        lax.fori_loop(0, ZS // 2, pair, 0)
         own = pl.ds(pl.multiple_of(me_t * RANK, RANK), RANK)
         code_in[phase, own, :] = code_out[phase, own, :]
 

time: 122 us -> 122 us (level)
  no operation moved by 1% of the time
where the time goes in v3:
time: 122 us
  Pallas kernels  120 us (98%)
  local copies, waits for them, and re-layouts  1.41 us (1%)
    pallas_call x1, Pallas kernels, per_device(): pl.pallas_call(kernel, out_shape=(field, field), in_specs=[anywhere, anyw...  120 us

profile of v3, /device:TPU:1, one launch (start us, length us, event | category | flops | bytes accessed | tf_op | source)
XLA Modules:
  0.0 121.7 jit_solution(839488550576589730)
XLA Ops:
  0.6 119.7 %shard_map.77 = (f32[2,2,64,256]{3,2,1,0:T(8,128)S(1)}, f32[2,2,64,256]{3,2,1,0:T(8,128)S(1)}) custom-call(f32[2,2,64,256]{3,2,1,0:T(8,128)} %start_hbm.1, bf16[2,32,256,128]{3,2,1,0:T(8,128)(2,1)} %bitcast.11, bf16[2,32,256,128]{3,2,1,0:T(8,128)(2,1)} %bitcast.12, s32[2,32,32]{2,1,0:T(8,128)} %rank_ref.1, s32[2,128]{1,0:T(2,128)} %bitcast.13, ...), custom_call_target="tpu_custom_call" | custom-call | tf_op jit(solution)/shard_map/pallas_call | solution.py:288
  120.3 0.7 copy.12
  121.0 0.7 copy.13

commit v4 on v3

--- a/solution.py
+++ b/solution.py
@@ -53,7 +53,7 @@
 def kernel(
     start_hbm, v_hbm, u_hbm, rank_ref, onset_ref, trig_hbm,
     focus_ref, up_ref,
-    start_ref, trig_ref, v_raw, u_raw, v_ref, u_ref, spread, stack, code_out, code_in, turned,
+    start_ref, trig_ref, v_raw, u_raw, v_ref, u_ref, spread, stack, code_out, code_in,
     wave_out, wave_in, gated_out, gated_in, table, gate_rows,
     load_sem, code_send, code_recv, wave_send, wave_recv, gated_send, gated_recv,
 ):
@@ -75,7 +75,7 @@
     load_u = pltpu.make_async_copy(u_hbm, u_raw, load_sem.at[1])
     load_start = pltpu.make_async_copy(start_hbm, start_ref, load_sem.at[2])
     load_trig = pltpu.make_async_copy(trig_hbm, trig_ref, load_sem.at[3])
-    for load in (load_start, load_v, load_trig, load_u):
+    for load in (load_start, load_v, load_trig):
         load.start()
 
     def set_stack(chunk, fields, forward):
@@ -104,12 +104,10 @@
                     left = part * TILE + side * HALF
                     factor_ref[band, rows, left : left + HALF] = piece
 
-    def send_codes(factor_ref, phase, chunk, prepare=None):
+    def send_codes(factor_ref, phase, chunk):
         def pair(index, carry):
             planes = ((me_z + ZS // 2 - index) % ZS, (me_z + ZS // 2 + 1 + index) % ZS)
             for z in planes:
-                if prepare is not None:
-                    prepare(z)
                 rows = pl.ds(pl.multiple_of(z * (XS * RANK), XS * RANK), XS * RANK)
                 product = contract(factor_ref[0, rows, :], stack[chunk, 0], 1, 1) + contract(
                     factor_ref[1, rows, :], stack[chunk, 1], 1, 1
@@ -124,7 +122,7 @@
                             src_ref=code_out.at[phase, pl.ds(pl.multiple_of(tile * RANK, RANK), RANK)],
                             dst_ref=code_in.at[phase, pl.ds(pl.multiple_of(me_t * RANK, RANK), RANK)],
                             send_sem=code_send.at[phase],
-                            recv_sem=code_recv.at[phase],
+                            recv_sem=code_recv.at[phase, index],
                             device_id=(me_f, tile),
                             device_id_type=MESH,
                         ).start()
@@ -143,13 +141,21 @@
         pltpu.make_async_copy(ref, ref, sem).wait()
 
     def image(factor_ref, phase, forward):
-        wait_bytes(code_in.at[phase, pl.ds(0, ROWS - RANK)], code_recv.at[phase])
-        turned[...] = code_in[phase].T
+        totals = [None, None]
+        for index in range(ZS // 2):
+            blocks = 2 * XS - (1 if index == ZS // 2 - 1 else 0)
+            wait_bytes(code_in.at[phase, pl.ds(0, blocks * RANK)], code_recv.at[phase, index])
+            for z in ((me_z + ZS // 2 + index) % ZS, (me_z + ZS // 2 - 1 - index) % ZS):
+                rows = pl.ds(pl.multiple_of(z * (XS * RANK), XS * RANK), XS * RANK)
+                turned = code_in[phase, rows, :].T
+                for band in range(2):
+                    term = contract(
+                        turned[band * 2 * SC : (band + 1) * 2 * SC, :], factor_ref[band, rows, :], 1, 0
+                    )
+                    totals[band] = term if totals[band] is None else totals[band] + term
         sign = 1.0 if forward else -1.0
         for band in range(2):
-            product = contract(
-                turned[band * 2 * SC : (band + 1) * 2 * SC, :], factor_ref[band], 1, 0
-            )
+            product = totals[band]
             real = product[:SC, :TILE] - sign * product[SC:, TILE:]
             imag = product[SC:, :TILE] + sign * product[:SC, TILE:]
             for group in range(GROUPS):
@@ -211,24 +217,26 @@
         rows = slice(chunk * SC, (chunk + 1) * SC)
         return [[start_ref[band, part, rows, :] for part in range(2)] for band in range(2)]
 
+    def prepare_v(z, carry):
+        for over in range(XS):
+            unpack(v_raw, v_ref, z * XS + over, over, lambda band, tile: rank_ref[band, tile, me_t])
+        return carry
+
     stack[...] = jnp.zeros_like(stack)
     load_start.wait()
     for chunk in range(CHUNKS):
         set_stack(chunk, start_fields(chunk), True)
     load_v.wait()
+    load_u.start()
+    lax.fori_loop(0, ZS, prepare_v, 0)
     pl.semaphore_wait(barrier, GROUPS + TILES - 2)
-
-    def prepare_v(z):
-        for over in range(XS):
-            unpack(v_raw, v_ref, z * XS + over, over, lambda band, tile: rank_ref[band, tile, me_t])
 
     def prepare_u(z, carry):
         for over in range(XS):
             unpack(u_raw, u_ref, z * XS + over, over, lambda band, tile: rank_ref[band, me_t, tile])
         return carry
 
-    send_codes(v_ref, 0, 0, prepare_v)
-    for chunk in range(1, CHUNKS):
+    for chunk in range(CHUNKS):
         send_codes(v_ref, chunk, chunk)
 
     load_trig.wait()
@@ -301,7 +309,6 @@
             pltpu.VMEM((CHUNKS, 2, 4 * SC, 2 * TILE), BF16),
             pltpu.VMEM((PHASES, ROWS, 4 * SC), BF16),
             pltpu.VMEM((PHASES, ROWS, 4 * SC), BF16),
-            pltpu.VMEM((4 * SC, ROWS), BF16),
             pltpu.VMEM((PHASES, GROUPS, 2, 16, HALF), BF16),
             pltpu.VMEM((PHASES, GROUPS, 2, 16, HALF), BF16),
             pltpu.VMEM((PHASES, GROUPS, 2, 16, HALF), BF16),
@@ -310,7 +317,7 @@
             pltpu.VMEM((2 * NF, 2, NF, HALF), F32),
             dma((4,)),
             dma((PHASES,)),
-            dma((PHASES,)),
+            dma((PHASES, ZS // 2)),
             dma((PHASES,)),
             dma((PHASES,)),
             dma((PHASES,)),

time: 122 us -> 123 us (level)
  no operation moved by 1% of the time
where the time goes in v4:
time: 123 us; the launch traced here: 122 us
  Pallas kernels  120 us (98%)
  local copies, waits for them, and re-layouts  1.41 us (1%)
    pallas_call x1, Pallas kernels, per_device(): pl.pallas_call(kernel, out_shape=(field, field), in_specs=[anywhere, anyw...  120 us

profile of v4, /device:TPU:1, one launch (start us, length us, event | category | flops | bytes accessed | tf_op | source)
XLA Modules:
  0.0 122.5 jit_solution(5022780315042292614)
XLA Ops:
  0.6 120.4 %shard_map.77 = (f32[2,2,64,256]{3,2,1,0:T(8,128)S(1)}, f32[2,2,64,256]{3,2,1,0:T(8,128)S(1)}) custom-call(f32[2,2,64,256]{3,2,1,0:T(8,128)} %start_hbm.1, bf16[2,32,256,128]{3,2,1,0:T(8,128)(2,1)} %bitcast.11, bf16[2,32,256,128]{3,2,1,0:T(8,128)(2,1)} %bitcast.12, s32[2,32,32]{2,1,0:T(8,128)} %rank_ref.1, s32[2,128]{1,0:T(2,128)} %bitcast.13, ...), custom_call_target="tpu_custom_call" | custom-call | tf_op jit(solution)/shard_map/pallas_call | solution.py:296
  121.1 0.7 copy.12
  121.8 0.7 copy.13
